TPU v7x, 128 devices: a whole 4x4x4 slice. The times are simulated.
128 devices in a mesh: group: 8 (over z, core), shard: 8 (over y_lo, x), side: 2 (over y_hi).
Axes of the slice: x: 4, y: 4 (y_hi: 2, y_lo: 2; y = y_hi * 2 + y_lo), z: 4, core: 2. Of those that a mesh axis runs over, the one named last changes fastest.
Arguments:
- master: float32 [64, 2048, 768], P('group', ('shard', 'side')), may hold values from -0.125 to 0.125
- momentum: float32 [64, 2048, 768], P('group', ('shard', 'side')), may hold values from -24 to 24
- gradient: bfloat16 [64, 2048, 768], P('group', ('shard', 'side')), may hold values from -6 to 6
- up_weight: bfloat16 [64, 768, 2048], P(('group', 'shard'), 'side'), may hold values from -0.125 to 0.125
- down_weight: bfloat16 [64, 768, 2048], P(('group', 'shard'), 'side'), may hold values from -0.21875 to 0.21875
- tokens: bfloat16 [512, 2048], replicated, may hold values from -6 to 6
- routes: int32 [512, 8], replicated, may hold values from 0 to 63, all different within a row; in each aligned block of 512 rows (0 to 511, 512 to 1023, ...) at most 128 rows name the same one
- route_weight: float32 [512, 8], replicated, may hold values from 0.1 to 1
Outputs:
- new_master: float32 [64, 2048, 768], P('group', ('shard', 'side'))
- new_momentum: float32 [64, 2048, 768], P('group', ('shard', 'side'))
- combined: bfloat16 [512, 2048], P(('group', 'shard', 'side'))
Inputs may be any that keep to these rules, and one draw needn't show every extreme that they name: `routes`: each row names 8 different experts; no expert is named by more than 128 rows, a bound that some block reaches; every expert is named by some row.
All inputs are finite; a program needn't handle non-finite values.
Results may differ from a plain program's by a relative error of at most 0.02.
Values may be sent and summed in bfloat16 or wider, within the bound.
A program may use at most 128 MiB of HBM per device.

v0:
```python
import functools
import math

import jax
import jax.numpy as jnp
from jax import lax
from jax.experimental import pallas as pl
from jax.experimental.pallas import tpu as pltpu
from jax.sharding import PartitionSpec as P

NS_ITERS = 5
CAP = 128
MOMENTUM_BETA = 0.95
LEARN_RATE = 0.08
WEIGHT_DECAY = 0.1
NEWTON_A = 3.4445
NEWTON_B = -4.775
NEWTON_C = 2.0315
EPSILON = 1e-07
MESH = pl.DeviceIdType.MESH
F32 = jnp.float32
BF16 = jnp.bfloat16


def dot(a, b):
    return jnp.dot(a, b, preferred_element_type=F32)


def kernel(
    dims,
    master, momentum, gradient, up_hbm, down_hbm, tokens_hbm, routes, route_weight,
    out_master, out_momentum, out_combined,
    mom, grad, mast, sbuf, xbuf, mhalf, mbuf, obuf, osend,
    rf, rb, mb, tf, tb, qf, qb, tx, gx, gsend,
    upw, downw, tok, tok_o, tok_r, upv, hid, weight,
    e1own, e1send, e1recv, e2send, e2recv, e3send, e3recv, comb,
    ld_m, ld_g, ld_x, ld_w, st_m, st_x, st_c,
    a_send, a_recv, f_send, f_recv, d_send, d_recv, c_send, c_recv,
    t_send, t_recv, e1_s, e1_r, e2_s, e2_r, e3_s, e3_r,
):
    NZ, NS, ROWS, F, D, T = dims
    H = F // 2
    NP = 2 * NS
    TB = T // (2 * NZ)
    RB = TB // NP
    gi = lax.axis_index("group")
    z, k = gi // 2, gi % 2
    s = lax.axis_index("shard")
    a = lax.axis_index("side")
    same = a == k
    differ = a != k
    mine = s * 2 + a
    pgroup, pside = z * 2 + a, k
    sibling = {"group": z * 2 + 1 - k, "shard": s, "side": a}
    swap = {"group": z * 2 + 1 - k, "shard": s, "side": 1 - a}

    def remote(src, dst, send, recv, device):
        return pltpu.make_async_remote_copy(
            src_ref=src, dst_ref=dst, send_sem=send, recv_sem=recv,
            device_id=device, device_id_type=MESH,
        )

    def rows_of(r):
        return pl.ds(pl.multiple_of(r * ROWS, ROWS), ROWS)

    def load(j):
        pltpu.make_async_copy(momentum.at[j], mom.at[j], ld_m.at[j]).start()
        pltpu.make_async_copy(gradient.at[j], grad.at[j], ld_g.at[j]).start()

    def turn(t):
        return lax.rem(s + 1 + t, NS)

    def origin(t):
        return lax.rem(s + 2 * NS - 1 - t, NS)

    @pl.loop(0, NS)
    def _(t):
        load(turn(t))

    w_loads = [
        pltpu.make_async_copy(tokens_hbm, tok, ld_w.at[0]),
        pltpu.make_async_copy(up_hbm.at[0], upw, ld_w.at[1]),
        pltpu.make_async_copy(down_hbm.at[0], downw, ld_w.at[2]),
    ]

    barrier = pltpu.get_barrier_semaphore()

    def greet(device):
        pl.semaphore_signal(barrier, inc=1, device_id=device, device_id_type=MESH)

    @pl.loop(1, NP)
    def _(i):
        r = lax.rem(mine + i, NP)
        greet({"group": gi, "shard": r // 2, "side": lax.rem(r, 2)})

    @pl.loop(1, NZ)
    def _(i):
        greet({"group": lax.rem(z + i, NZ) * 2 + k, "shard": s, "side": a})

    greet(sibling)

    @pl.when(differ)
    def _():
        @pl.loop(0, NS)
        def _(j):
            greet({"group": pgroup, "shard": j, "side": pside})

        pl.semaphore_wait(barrier, NP - 1 + NZ - 1 + 1 + NS)

    @pl.when(same)
    def _():
        pl.semaphore_wait(barrier, NP - 1 + NZ - 1 + 1)

    def a_copy(j):
        return remote(
            sbuf.at[j], xbuf.at[rows_of(mine)], a_send.at[j], a_recv.at[s],
            {"group": pgroup, "shard": j, "side": pside},
        )

    @pl.loop(0, NS)
    def _(t):
        j = turn(t)
        pltpu.make_async_copy(momentum.at[j], mom.at[j], ld_m.at[j]).wait()
        pltpu.make_async_copy(gradient.at[j], grad.at[j], ld_g.at[j]).wait()
        g = grad[j].astype(F32)
        m = MOMENTUM_BETA * mom[j] + g
        mom[j] = m
        sbuf[j] = (g + MOMENTUM_BETA * m).astype(BF16)
        own = jnp.logical_and(same, j == s)

        @pl.when(own)
        def _():
            xbuf[rows_of(mine), :] = sbuf[j]

        @pl.when(jnp.logical_not(own))
        def _():
            a_copy(j).start()

        pltpu.make_async_copy(mom.at[j], out_momentum.at[j], st_m.at[j]).start()

    for c in w_loads:
        c.start()

    @pl.loop(0, NS)
    def _(t):
        j = turn(t)
        pltpu.make_async_copy(master.at[j], mast.at[j], ld_x.at[j]).start()

    for c in w_loads:
        c.wait()
    token_row = lax.broadcasted_iota(jnp.int32, (T, T), 0)
    token_col = lax.broadcasted_iota(jnp.int32, (T, T), 1)
    lower = jnp.where(token_col <= token_row, 1.0, 0.0).astype(BF16)

    def slots(expert):
        hit = routes[...] == expert
        member = jnp.max(jnp.where(hit, 1.0, 0.0), axis=1, keepdims=True)
        wide = jnp.broadcast_to(member, (T, CAP))
        rank = dot(lower, wide.astype(BF16))
        slot = lax.broadcasted_iota(jnp.int32, (T, CAP), 1).astype(F32) + 1.0
        chosen = jnp.where(jnp.logical_and(rank == slot, wide > 0.5), 1.0, 0.0)
        return chosen.astype(BF16), hit

    def pick(chosen):
        return lax.dot_general(
            chosen, tok[...], (((0,), (0,)), ((), ())), preferred_element_type=F32
        ).astype(BF16)

    chosen_o, _ = slots((z * 2 + a) * NS + s)
    tok_o[...] = pick(chosen_o)
    chosen_r, hit_r = slots(gi * NS + s)
    tok_r[...] = pick(chosen_r)
    weight[...] = jnp.broadcast_to(
        jnp.sum(jnp.where(hit_r, route_weight[...], 0.0), axis=1, keepdims=True), (T, 128)
    )
    upv[...] = lax.dot_general(
        tok_r[...], upw[...], (((1,), (1,)), ((), ())), preferred_element_type=F32
    )

    @pl.loop(0, NS)
    def _(t):
        j = turn(t)
        pltpu.make_async_copy(master.at[j], mast.at[j], ld_x.at[j]).wait()
        half = mast[j].astype(BF16)
        mhalf[j, 0] = half[:, :H]
        mhalf[j, 1] = half[:, H:]

    rf[...] = jnp.zeros_like(rf)
    tx[...] = jnp.zeros_like(tx)

    def f_copy(o, core):
        block = rows_of(o * 2 + core)
        return remote(xbuf.at[block], xbuf.at[block], f_send.at[o], f_recv.at[o], sibling)

    def gram(o):
        f_copy(o, 1 - k).wait_recv()
        pair = pl.ds(pl.multiple_of(o * 2 * ROWS, 2 * ROWS), 2 * ROWS)
        x = xbuf[pair, :]
        rf[...] += lax.dot_general(
            x, x, (((0,), (0,)), ((), ())), preferred_element_type=F32
        )
        tx[...] += dot(tok_o[:, pair], x)

    @pl.loop(0, NS)
    def _(t):
        o = origin(t)

        @pl.when(jnp.logical_not(jnp.logical_and(same, o == s)))
        def _():
            remote(
                sbuf.at[o], xbuf.at[rows_of(o * 2 + k)], a_send.at[o], a_recv.at[o],
                {"group": pgroup, "shard": o, "side": pside},
            ).wait_recv()

        f_copy(o, k).start()

        @pl.when(t > 0)
        def _():
            gram(origin(t - 1))

    gram(origin(NS - 1))

    def d_copy(j, h):
        return remote(
            mhalf.at[j, h], mbuf.at[rows_of(mine)], d_send.at[j * 2 + h], d_recv.at[mine],
            {"group": gi, "shard": j, "side": h},
        )

    @pl.loop(0, NP)
    def _(i):
        r = lax.rem(mine + i, NP)
        j, h = r // 2, lax.rem(r, 2)

        @pl.when(i == 0)
        def _():
            mbuf[rows_of(mine), :] = mhalf[j, h]

        @pl.when(i > 0)
        def _():
            d_copy(j, h).start()

    B = 128
    eye = lax.broadcasted_iota(jnp.int32, (B, B), 0) == lax.broadcasted_iota(jnp.int32, (B, B), 1)
    blocks = [pl.ds(i * B, B) for i in range(F // B)]
    halves = [pl.ds(0, H), pl.ds(H, H)]

    def trace_of_rf():
        total = jnp.zeros((B, B), F32)
        for b in blocks:
            total = total + jnp.where(eye, rf[b, b], 0.0)
        return jnp.sum(total)

    def shift_rf(d):
        for b in blocks:
            v = rf[b, b] - jnp.where(eye, d, 0.0)
            rf[b, b] = v
            rb[b, b] = v.astype(BF16)

    scale = jnp.sqrt(trace_of_rf() + jnp.zeros((1, 1), F32))[0, 0]
    inverse = (1.0 / (jnp.zeros((1, 1), F32) + scale + EPSILON))[0, 0]
    for h in halves:
        v = rf[h, :] * inverse * inverse
        rf[h, :] = v
        rb[h, :] = v.astype(BF16)

    def recenter(d):
        move = trace_of_rf() * (1.0 / F)
        shift_rf(move)
        return d + move

    def form_mix(d):
        e1 = NEWTON_B + 2.0 * NEWTON_C * d
        for h in halves:
            mb[h, :] = (e1 * rf[h, :] + NEWTON_C * dot(rb[h, :], rb[...])).astype(BF16)
        return NEWTON_A + NEWTON_B * d + NEWTON_C * d * d

    def grow_q(lead, q):
        for h in halves:
            v = lead * qf[h, :] + q * mb[h, :].astype(F32) + dot(qb[h, :], mb[...])
            qf[h, :] = v
            qb[h, :] = v.astype(BF16)
        return q * lead

    def grow_g(lead, d):
        for h in halves:
            v = lead * rf[h, :] + d * mb[h, :].astype(F32) + dot(rb[h, :], mb[...])
            tf[h, :] = v
            tb[h, :] = v.astype(BF16)
        t = lead * d
        for h in halves:
            v = lead * tf[h, :] + t * mb[h, :].astype(F32) + dot(tb[h, :], mb[...])
            rf[h, :] = v
            rb[h, :] = v.astype(BF16)
        return lead * t

    d = recenter(jnp.float32(0.0))
    lead = form_mix(d)
    q = lead
    qf[...] = mb[...].astype(F32)
    qb[...] = mb[...]
    d = grow_g(lead, d)

    def iteration(_, carry):
        d, q = carry
        d = recenter(d)
        lead = form_mix(d)
        q = grow_q(lead, q)
        d = grow_g(lead, d)
        return d, q

    d, q = lax.fori_loop(1, NS_ITERS - 1, iteration, (d, q))
    d = recenter(d)
    lead = form_mix(d)
    q = grow_q(lead, q)

    cols = pl.ds(pl.multiple_of(k * H, H), H)
    part = inverse * (q * tx[:, cols] + dot(tx[...].astype(BF16), qb[:, cols]))
    t_copy = remote(gsend, gx, t_send, t_recv, swap)

    @pl.when(same)
    def _():
        gx[...] = part.astype(BF16)

    @pl.when(differ)
    def _():
        gsend[...] = part.astype(BF16)
        t_copy.start()

    def c_copy(o):
        return remote(
            osend.at[o], obuf.at[s], c_send.at[o], c_recv.at[s],
            {"group": pgroup, "shard": o, "side": pside},
        )

    BUNCH = min(4, NS)
    for first in range(0, NS, BUNCH):
        who = [turn(first + i) for i in range(BUNCH)]
        x = jnp.concatenate([xbuf[rows_of(o * 2 + k), :] for o in who], axis=0)
        y = (inverse * (q * x.astype(F32) + dot(x, qb[...]))).astype(BF16)
        for i, o in enumerate(who):
            osend[o] = y[i * ROWS:(i + 1) * ROWS]
            own = jnp.logical_and(same, o == s)

            @pl.when(own)
            def _():
                obuf[s] = osend[o]

            @pl.when(jnp.logical_not(own))
            def _():
                c_copy(o).start()

    @pl.loop(1, NP)
    def _(i):
        r = lax.rem(mine + i, NP)
        remote(
            mhalf.at[r // 2, lax.rem(r, 2)], mbuf.at[rows_of(r)], d_send.at[r], d_recv.at[r],
            {"group": gi, "shard": r // 2, "side": lax.rem(r, 2)},
        ).wait_recv()

    decay = 1.0 - LEARN_RATE * WEIGHT_DECAY
    step_scale = LEARN_RATE * 0.2 * math.sqrt(max(D, F))
    kept = decay * dot(tok_r[...], mbuf[...])

    @pl.when(differ)
    def _():
        t_copy.wait_recv()

    gate = kept - step_scale * gx[...].astype(F32)
    hidden = (gate * (1.0 / (1.0 + jnp.exp(-gate))) * upv[...]).astype(BF16)
    hid[...] = dot(chosen_r, hidden).astype(BF16)

    def share(core):
        parts = [pl.ds(pl.multiple_of((i * 2 + core) * TB, TB), TB) for i in range(NZ)]
        rows = jnp.concatenate([hid[p, :] for p in parts], axis=0)
        value = dot(rows, downw[...])
        scale = jnp.concatenate([weight[p, :1] for p in parts], axis=0)
        return value * scale

    away = share(1 - k).astype(BF16)
    for i in range(NZ):
        e1send[i] = away[i * TB:(i + 1) * TB]
    e1_copy = remote(e1send, e1recv, e1_s, e1_r, sibling)
    e1_copy.start()
    home = share(k)
    for i in range(NZ):
        e1own[i] = home[i * TB:(i + 1) * TB]
    e1_copy.wait_recv()

    def e2_copy(i):
        return remote(
            e2send.at[i], e2recv.at[i], e2_s.at[i], e2_r.at[i],
            {"group": lax.rem(z + 1 + i, NZ) * 2 + k, "shard": s, "side": a},
        )

    @pl.loop(0, NZ - 1)
    def _(i):
        to = lax.rem(z + 1 + i, NZ)
        e2send[i] = (e1own[to] + e1recv[to].astype(F32)).astype(BF16)
        e2_copy(i).start()

    total = e1own[z] + e1recv[z].astype(F32)
    for i in range(NZ - 1):
        e2_copy(i).wait_recv()
        total = total + e2recv[i].astype(F32)
    for r in range(NP):
        e3send[r] = total[r * RB:(r + 1) * RB].astype(BF16)

    def e3_copy(r, slot):
        return remote(
            e3send.at[r], e3recv.at[slot], e3_s.at[r], e3_r.at[slot],
            {"group": gi, "shard": r // 2, "side": lax.rem(r, 2)},
        )

    @pl.loop(1, NP)
    def _(i):
        e3_copy(lax.rem(mine + i, NP), mine).start()

    e3recv[mine] = e3send[mine]

    @pl.loop(0, NS)
    def _(t):
        o = origin(t)

        @pl.when(jnp.logical_not(jnp.logical_and(same, o == s)))
        def _():
            remote(
                osend.at[o], obuf.at[o], c_send.at[o], c_recv.at[o],
                {"group": pgroup, "shard": o, "side": pside},
            ).wait_recv()

        mast[o] = decay * mast[o] - step_scale * obuf[o].astype(F32)
        pltpu.make_async_copy(mast.at[o], out_master.at[o], st_x.at[o]).start()

    @pl.loop(1, NP)
    def _(i):
        r = lax.rem(mine + i, NP)
        e3_copy(r, r).wait_recv()

    final = e3recv[0].astype(F32)
    for r in range(1, NP):
        final = final + e3recv[r].astype(F32)
    comb[...] = final.astype(BF16)
    last = pltpu.make_async_copy(comb, out_combined, st_c)
    last.start()

    @pl.loop(0, NS)
    def _(t):
        j = turn(t)

        @pl.when(jnp.logical_not(jnp.logical_and(same, j == s)))
        def _():
            a_copy(j).wait_send()
            c_copy(j).wait_send()

        f_copy(j, k).wait_send()
        pltpu.make_async_copy(mom.at[j], out_momentum.at[j], st_m.at[j]).wait()
        pltpu.make_async_copy(mast.at[j], out_master.at[j], st_x.at[j]).wait()

    @pl.loop(1, NP)
    def _(i):
        r = lax.rem(mine + i, NP)
        d_copy(r // 2, lax.rem(r, 2)).wait_send()
        e3_copy(r, mine).wait_send()

    @pl.loop(0, NZ - 1)
    def _(i):
        e2_copy(i).wait_send()

    e1_copy.wait_send()

    @pl.when(differ)
    def _():
        t_copy.wait_send()

    last.wait()


def body(master, momentum, gradient, up_weight, down_weight, tokens, routes, route_weight):
    NS, ROWS, F = master.shape
    NZ = lax.axis_size("group") // 2
    T, D = tokens.shape
    H = F // 2
    NP = 2 * NS
    TB = T // (2 * NZ)
    RB = TB // NP
    dma = pltpu.SemaphoreType.DMA
    vmem = pltpu.VMEM
    scratch = dict(
        mom=vmem((NS, ROWS, F), F32), grad=vmem((NS, ROWS, F), BF16), mast=vmem((NS, ROWS, F), F32),
        sbuf=vmem((NS, ROWS, F), BF16), xbuf=vmem((D, F), BF16), mhalf=vmem((NS, 2, ROWS, H), BF16),
        mbuf=vmem((D, H), BF16), obuf=vmem((NS, ROWS, F), BF16), osend=vmem((NS, ROWS, F), BF16),
        rf=vmem((F, F), F32), rb=vmem((F, F), BF16), mb=vmem((F, F), BF16), tf=vmem((F, F), F32),
        tb=vmem((F, F), BF16), qf=vmem((F, F), F32), qb=vmem((F, F), BF16), tx=vmem((CAP, F), F32),
        gx=vmem((CAP, H), BF16), gsend=vmem((CAP, H), BF16),
        upw=vmem((H, D), BF16), downw=vmem((H, D), BF16), tok=vmem((T, D), BF16),
        tok_o=vmem((CAP, D), BF16), tok_r=vmem((CAP, D), BF16), upv=vmem((CAP, H), F32),
        hid=vmem((T, H), BF16), weight=vmem((T, 128), F32),
        e1own=vmem((NZ, TB, D), F32), e1send=vmem((NZ, TB, D), BF16), e1recv=vmem((NZ, TB, D), BF16),
        e2send=vmem((NZ - 1, TB, D), BF16), e2recv=vmem((NZ - 1, TB, D), BF16),
        e3send=vmem((NP, RB, D), BF16), e3recv=vmem((NP, RB, D), BF16), comb=vmem((RB, D), BF16),
        ld_m=dma((NS,)), ld_g=dma((NS,)), ld_x=dma((NS,)), ld_w=dma((3,)),
        st_m=dma((NS,)), st_x=dma((NS,)), st_c=dma,
        a_send=dma((NS,)), a_recv=dma((NS,)), f_send=dma((NS,)), f_recv=dma((NS,)),
        d_send=dma((NP,)), d_recv=dma((NP,)), c_send=dma((NS,)), c_recv=dma((NS,)),
        t_send=dma, t_recv=dma, e1_s=dma, e1_r=dma,
        e2_s=dma((NZ - 1,)), e2_r=dma((NZ - 1,)), e3_s=dma((NP,)), e3_r=dma((NP,)),
    )
    hbm = pl.BlockSpec(memory_space=pl.ANY)
    local = pl.BlockSpec(memory_space=pltpu.VMEM)
    return pl.pallas_call(
        functools.partial(kernel, (NZ, NS, ROWS, F, D, T)),
        out_shape=(
            jax.ShapeDtypeStruct(master.shape, F32),
            jax.ShapeDtypeStruct(master.shape, F32),
            jax.ShapeDtypeStruct((RB, D), BF16),
        ),
        in_specs=[hbm] * 6 + [local] * 2,
        out_specs=[hbm] * 3,
        scratch_shapes=list(scratch.values()),
        compiler_params=pltpu.CompilerParams(
            collective_id=0, has_side_effects=True, vmem_limit_bytes=60 * 1024 * 1024
        ),
        name="muon_rollout",
    )(master, momentum, gradient, up_weight, down_weight, tokens, routes, route_weight)


def solution(mesh):
    in_specs = (
        P("group", ("shard", "side"), None),
        P("group", ("shard", "side"), None),
        P("group", ("shard", "side"), None),
        P(("group", "shard"), "side", None),
        P(("group", "shard"), "side", None),
        P(),
        P(),
        P(),
    )
    out_specs = (
        P("group", ("shard", "side"), None),
        P("group", ("shard", "side"), None),
        P(("group", "shard", "side"), None),
    )
    return jax.shard_map(body, mesh=mesh, in_specs=in_specs, out_specs=out_specs, check_vma=False)
```

profile of v0, /device:TPU:1, one launch (start us, length us, event | category | flops | bytes accessed | tf_op | source)
XLA Modules:
  0.0 98.9 jit_solution(15651581910177515064)
XLA Ops:
  0.6 1.6 %copy.11.routes = s32[512,8]{1,0:T(8,128)} copy(s32[512,8]{0,1:T(8,128)} %param.14) | data formatting | bytes 32768 | tf_op args[6]
  2.2 1.6 %copy.12.route_weight = f32[512,8]{1,0:T(8,128)} copy(f32[512,8]{0,1:T(8,128)} %param.15) | data formatting | bytes 32768 | tf_op args[7]
  3.7 88.9 %muon_rollout.1 = (f32[8,128,768]{2,1,0:T(8,128)}, f32[8,128,768]{2,1,0:T(8,128)}, bf16[4,2048]{1,0:T(4,128)(2,1)}) custom-call(f32[8,128,768]{2,1,0:T(8,128)} %master.1, f32[8,128,768]{2,1,0:T(8,128)} %momentum.1, bf16[8,128,768]{2,1,0:T(8,128)(2,1)} %gradient.1, bf16[1,384,2048]{2,1,0:T(8,128)(2,1)} %up_hbm.1, bf16[1,384,2048]{2,1,0:T(8,128)(2,1)} %down_hbm.1, ...), custom_call_target="tpu_custom_call" | custom-call | tf_op jit(solution)/shard_map/muon_rollout/pallas_call | solution.py:510
  92.6 0.0 copy-start
  92.7 3.9 %copy.16 = f32[8,128,768]{2,1,0:T(8,128)} copy(f32[8,128,768]{2,1,0:T(8,128)} %get-tuple-element.6) | data formatting | bytes 6291456
  96.6 0.0 copy-done
  96.6 0.0 copy-start.1
  96.6 1.7 %copy.17 = f32[8,128,768]{2,1,0:T(8,128)} copy(f32[8,128,768]{2,1,0:T(8,128)S(1)} %copy-done) | data formatting | bytes 6291456
  98.3 0.0 copy-done.1
  98.3 0.6 copy.18
Async XLA Ops:
  92.6 4.0 %copy-start = (f32[8,128,768]{2,1,0:T(8,128)S(1)}, f32[8,128,768]{2,1,0:T(8,128)}, u32[]{:S(2)}) copy-start(f32[8,128,768]{2,1,0:T(8,128)} %get-tuple-element.7) | copy-start | bytes 9437188
  96.6 1.7 %copy-start.1 = (bf16[4,2048]{1,0:T(4,128)(2,1)S(1)}, bf16[4,2048]{1,0:T(4,128)(2,1)}, u32[]{:S(2)}) copy-start(bf16[4,2048]{1,0:T(4,128)(2,1)} %get-tuple-element.8) | copy-start | bytes 49156
where the time goes:
time: 99.1 us; the launch traced here: 98.9 us
  Pallas kernels  88.9 us (90%)
  local copies, waits for them, and re-layouts  9.32 us (9%)
    pallas_call x1, Pallas kernels, body(): pl.pallas_call(functools.partial(kernel, (NZ, NS, ROWS, F, D, T)), out_sh...  88.9 us
    unnamed x9, local copies, waits for them, and re-layouts  9.32 us

commit v1 on v0

--- a/solution.py
+++ b/solution.py
@@ -29,12 +29,12 @@
 def kernel(
     dims,
     master, momentum, gradient, up_hbm, down_hbm, tokens_hbm, routes, route_weight,
-    out_master, out_momentum, out_combined,
-    mom, grad, mast, sbuf, xbuf, mhalf, mbuf, obuf, osend,
+    mast, mom, comb,
+    grad, sbuf, xbuf, mhalf, mbuf, obuf, osend,
     rf, rb, mb, tf, tb, qf, qb, tx, gx, gsend,
-    upw, downw, tok, tok_o, tok_r, upv, hid, weight,
-    e1own, e1send, e1recv, e2send, e2recv, e3send, e3recv, comb,
-    ld_m, ld_g, ld_x, ld_w, st_m, st_x, st_c,
+    upw, downw, tok, tok_o, tok_r, upv, hid, chosen,
+    e1own, e1send, e1recv, e2send, e2recv, e3send, e3recv,
+    ld_m, ld_g, ld_x, ld_w,
     a_send, a_recv, f_send, f_recv, d_send, d_recv, c_send, c_recv,
     t_send, t_recv, e1_s, e1_r, e2_s, e2_r, e3_s, e3_r,
 ):
@@ -136,8 +136,6 @@
         def _():
             a_copy(j).start()
 
-        pltpu.make_async_copy(mom.at[j], out_momentum.at[j], st_m.at[j]).start()
-
     for c in w_loads:
         c.start()
 
@@ -150,30 +148,24 @@
         c.wait()
     token_row = lax.broadcasted_iota(jnp.int32, (T, T), 0)
     token_col = lax.broadcasted_iota(jnp.int32, (T, T), 1)
-    lower = jnp.where(token_col <= token_row, 1.0, 0.0).astype(BF16)
+    upper = jnp.where(token_row <= token_col, 1.0, 0.0).astype(BF16)
 
     def slots(expert):
         hit = routes[...] == expert
-        member = jnp.max(jnp.where(hit, 1.0, 0.0), axis=1, keepdims=True)
-        wide = jnp.broadcast_to(member, (T, CAP))
-        rank = dot(lower, wide.astype(BF16))
-        slot = lax.broadcasted_iota(jnp.int32, (T, CAP), 1).astype(F32) + 1.0
-        chosen = jnp.where(jnp.logical_and(rank == slot, wide > 0.5), 1.0, 0.0)
-        return chosen.astype(BF16), hit
-
-    def pick(chosen):
-        return lax.dot_general(
-            chosen, tok[...], (((0,), (0,)), ((), ())), preferred_element_type=F32
-        ).astype(BF16)
+        member = jnp.max(jnp.where(hit, 1.0, 0.0), axis=0, keepdims=True)
+        rank = dot(jnp.broadcast_to(member, (16, T)).astype(BF16), upper)[:1]
+        place = jnp.where(member > 0.5, rank - 1.0, -1.0)
+        slot = lax.broadcasted_iota(jnp.int32, (CAP, T), 0).astype(F32)
+        return jnp.where(slot == place, 1.0, 0.0), hit
 
     chosen_o, _ = slots((z * 2 + a) * NS + s)
-    tok_o[...] = pick(chosen_o)
+    tok_o[...] = dot(chosen_o.astype(BF16), tok[...]).astype(BF16)
     chosen_r, hit_r = slots(gi * NS + s)
-    tok_r[...] = pick(chosen_r)
-    weight[...] = jnp.broadcast_to(
-        jnp.sum(jnp.where(hit_r, route_weight[...], 0.0), axis=1, keepdims=True), (T, 128)
-    )
-    upv[...] = lax.dot_general(
+    tok_r[...] = dot(chosen_r.astype(BF16), tok[...]).astype(BF16)
+    weight = jnp.sum(jnp.where(hit_r, route_weight[...], 0.0), axis=0, keepdims=True)
+    weight = jnp.sum(chosen_r * weight, axis=1, keepdims=True)
+    chosen[...] = chosen_r.astype(BF16)
+    upv[...] = weight * lax.dot_general(
         tok_r[...], upw[...], (((1,), (1,)), ((), ())), preferred_element_type=F32
     )
 
@@ -367,14 +359,14 @@
 
     gate = kept - step_scale * gx[...].astype(F32)
     hidden = (gate * (1.0 / (1.0 + jnp.exp(-gate))) * upv[...]).astype(BF16)
-    hid[...] = dot(chosen_r, hidden).astype(BF16)
+    hid[...] = lax.dot_general(
+        chosen[...], hidden, (((0,), (0,)), ((), ())), preferred_element_type=F32
+    ).astype(BF16)
 
     def share(core):
         parts = [pl.ds(pl.multiple_of((i * 2 + core) * TB, TB), TB) for i in range(NZ)]
         rows = jnp.concatenate([hid[p, :] for p in parts], axis=0)
-        value = dot(rows, downw[...])
-        scale = jnp.concatenate([weight[p, :1] for p in parts], axis=0)
-        return value * scale
+        return dot(rows, downw[...])
 
     away = share(1 - k).astype(BF16)
     for i in range(NZ):
@@ -429,7 +421,6 @@
             ).wait_recv()
 
         mast[o] = decay * mast[o] - step_scale * obuf[o].astype(F32)
-        pltpu.make_async_copy(mast.at[o], out_master.at[o], st_x.at[o]).start()
 
     @pl.loop(1, NP)
     def _(i):
@@ -440,8 +431,6 @@
     for r in range(1, NP):
         final = final + e3recv[r].astype(F32)
     comb[...] = final.astype(BF16)
-    last = pltpu.make_async_copy(comb, out_combined, st_c)
-    last.start()
 
     @pl.loop(0, NS)
     def _(t):
@@ -453,8 +442,6 @@
             c_copy(j).wait_send()
 
         f_copy(j, k).wait_send()
-        pltpu.make_async_copy(mom.at[j], out_momentum.at[j], st_m.at[j]).wait()
-        pltpu.make_async_copy(mast.at[j], out_master.at[j], st_x.at[j]).wait()
 
     @pl.loop(1, NP)
     def _(i):
@@ -472,7 +459,13 @@
     def _():
         t_copy.wait_send()
 
-    last.wait()
+
+def hand_over(*refs):
+    copies = [pltpu.make_async_copy(refs[i], refs[3 + i], refs[6].at[i]) for i in range(3)]
+    for c in copies:
+        c.start()
+    for c in copies:
+        c.wait()
 
 
 def body(master, momentum, gradient, up_weight, down_weight, tokens, routes, route_weight):
@@ -486,7 +479,7 @@
     dma = pltpu.SemaphoreType.DMA
     vmem = pltpu.VMEM
     scratch = dict(
-        mom=vmem((NS, ROWS, F), F32), grad=vmem((NS, ROWS, F), BF16), mast=vmem((NS, ROWS, F), F32),
+        grad=vmem((NS, ROWS, F), BF16),
         sbuf=vmem((NS, ROWS, F), BF16), xbuf=vmem((D, F), BF16), mhalf=vmem((NS, 2, ROWS, H), BF16),
         mbuf=vmem((D, H), BF16), obuf=vmem((NS, ROWS, F), BF16), osend=vmem((NS, ROWS, F), BF16),
         rf=vmem((F, F), F32), rb=vmem((F, F), BF16), mb=vmem((F, F), BF16), tf=vmem((F, F), F32),
@@ -494,12 +487,11 @@
         gx=vmem((CAP, H), BF16), gsend=vmem((CAP, H), BF16),
         upw=vmem((H, D), BF16), downw=vmem((H, D), BF16), tok=vmem((T, D), BF16),
         tok_o=vmem((CAP, D), BF16), tok_r=vmem((CAP, D), BF16), upv=vmem((CAP, H), F32),
-        hid=vmem((T, H), BF16), weight=vmem((T, 128), F32),
+        hid=vmem((T, H), BF16), chosen=vmem((CAP, T), BF16),
         e1own=vmem((NZ, TB, D), F32), e1send=vmem((NZ, TB, D), BF16), e1recv=vmem((NZ, TB, D), BF16),
         e2send=vmem((NZ - 1, TB, D), BF16), e2recv=vmem((NZ - 1, TB, D), BF16),
-        e3send=vmem((NP, RB, D), BF16), e3recv=vmem((NP, RB, D), BF16), comb=vmem((RB, D), BF16),
+        e3send=vmem((NP, RB, D), BF16), e3recv=vmem((NP, RB, D), BF16),
         ld_m=dma((NS,)), ld_g=dma((NS,)), ld_x=dma((NS,)), ld_w=dma((3,)),
-        st_m=dma((NS,)), st_x=dma((NS,)), st_c=dma,
         a_send=dma((NS,)), a_recv=dma((NS,)), f_send=dma((NS,)), f_recv=dma((NS,)),
         d_send=dma((NP,)), d_recv=dma((NP,)), c_send=dma((NS,)), c_recv=dma((NS,)),
         t_send=dma, t_recv=dma, e1_s=dma, e1_r=dma,
@@ -507,21 +499,30 @@
     )
     hbm = pl.BlockSpec(memory_space=pl.ANY)
     local = pl.BlockSpec(memory_space=pltpu.VMEM)
-    return pl.pallas_call(
+    outs = pl.pallas_call(
         functools.partial(kernel, (NZ, NS, ROWS, F, D, T)),
         out_shape=(
-            jax.ShapeDtypeStruct(master.shape, F32),
-            jax.ShapeDtypeStruct(master.shape, F32),
-            jax.ShapeDtypeStruct((RB, D), BF16),
+            vmem(master.shape, F32),
+            vmem(master.shape, F32),
+            vmem((RB, D), BF16),
         ),
         in_specs=[hbm] * 6 + [local] * 2,
-        out_specs=[hbm] * 3,
+        out_specs=[local] * 3,
         scratch_shapes=list(scratch.values()),
         compiler_params=pltpu.CompilerParams(
-            collective_id=0, has_side_effects=True, vmem_limit_bytes=60 * 1024 * 1024
+            collective_id=0, has_side_effects=True, vmem_limit_bytes=48 * 1024 * 1024
         ),
         name="muon_rollout",
-    )(master, momentum, gradient, up_weight, down_weight, tokens, routes, route_weight)
+    )(master, momentum, gradient, up_weight, down_weight, tokens, routes.T, route_weight.T)
+    return pl.pallas_call(
+        hand_over,
+        out_shape=tuple(jax.ShapeDtypeStruct(o.shape, o.dtype) for o in outs),
+        in_specs=[hbm] * 3,
+        out_specs=[hbm] * 3,
+        scratch_shapes=[dma((3,))],
+        compiler_params=pltpu.CompilerParams(vmem_limit_bytes=1024 * 1024),
+        name="hand_over",
+    )(*outs)
 
 
 def solution(mesh):

time: 99.1 us -> 91.9 us (0.927)
  local copies, waits for them, and re-layouts: 9.32 us -> 0 us
  Pallas kernels: 88.9 us -> 90.9 us
    unnamed x9 -> x0, local copies, waits for them, and re-layouts: 9.32 us -> none
    pallas_call x0 -> x1, Pallas kernels: none -> 2.73 us  [body(): pl.pallas_call(hand_over, out_shape=tuple((jax.ShapeDtypeStruct(o.shape,...]
where the time goes in v1:
time: 91.9 us; the launch traced here: 91.7 us
  Pallas kernels  90.9 us (99%)
    pallas_call x1, Pallas kernels, body(): pl.pallas_call(functools.partial(kernel, (NZ, NS, ROWS, F, D, T)), out_sh...  88.1 us
    pallas_call x1, Pallas kernels, body(): pl.pallas_call(hand_over, out_shape=tuple((jax.ShapeDtypeStruct(o.shape,...  2.73 us

profile of v1, /device:TPU:1, one launch (start us, length us, event | category | flops | bytes accessed | tf_op | source)
XLA Modules:
  0.0 91.7 jit_solution(4150706630139173765)
XLA Ops:
  0.6 88.1 %muon_rollout.1 = (f32[8,128,768]{2,1,0:T(8,128)S(1)}, f32[8,128,768]{2,1,0:T(8,128)S(1)}, bf16[4,2048]{1,0:T(4,128)(2,1)S(1)}) custom-call(f32[8,128,768]{2,1,0:T(8,128)} %master.1, f32[8,128,768]{2,1,0:T(8,128)} %momentum.1, bf16[8,128,768]{2,1,0:T(8,128)(2,1)} %gradient.1, bf16[1,384,2048]{2,1,0:T(8,128)(2,1)} %up_hbm.1, bf16[1,384,2048]{2,1,0:T(8,128)(2,1)} %down_hbm.1, ...), custom_call_target="tpu_custom_call" | custom-call | tf_op jit(solution)/shard_map/muon_rollout/pallas_call | solution.py:502
  88.8 2.7 %hand_over.1 = (f32[8,128,768]{2,1,0:T(8,128)}, f32[8,128,768]{2,1,0:T(8,128)}, bf16[4,2048]{1,0:T(4,128)(2,1)}) custom-call(f32[8,128,768]{2,1,0:T(8,128)S(1)} %get-tuple-element.6.refs_0_, f32[8,128,768]{2,1,0:T(8,128)S(1)} %get-tuple-element.7.refs_1_, bf16[4,2048]{1,0:T(4,128)(2,1)S(1)} %get-tuple-element.8.refs_2_), custom_call_target="tpu_custom_call" | custom-call | tf_op jit(solution)/shard_map/hand_over/pallas_call | solution.py:517

commit v2 on v1

--- a/solution.py
+++ b/solution.py
@@ -10,6 +10,7 @@
 
 NS_ITERS = 5
 CAP = 128
+CHUNKS = 2
 MOMENTUM_BETA = 0.95
 LEARN_RATE = 0.08
 WEIGHT_DECAY = 0.1
@@ -33,7 +34,7 @@
     grad, sbuf, xbuf, mhalf, mbuf, obuf, osend,
     rf, rb, mb, tf, tb, qf, qb, tx, gx, gsend,
     upw, downw, tok, tok_o, tok_r, upv, hid, chosen,
-    e1own, e1send, e1recv, e2send, e2recv, e3send, e3recv,
+    e1own, e1send, e1recv, e2send, e2recv, e2last, e2got, e3send, e3recv,
     ld_m, ld_g, ld_x, ld_w,
     a_send, a_recv, f_send, f_recv, d_send, d_recv, c_send, c_recv,
     t_send, t_recv, e1_s, e1_r, e2_s, e2_r, e3_s, e3_r,
@@ -67,11 +68,37 @@
         pltpu.make_async_copy(momentum.at[j], mom.at[j], ld_m.at[j]).start()
         pltpu.make_async_copy(gradient.at[j], grad.at[j], ld_g.at[j]).start()
 
+    NX = 4 if NS % 4 == 0 else NS
+    NY = NS // NX
+    cx, cy = lax.rem(s, NX), a * NY + s // NX
+
+    def hop(t, sign):
+        if NX != 4:
+            return lax.rem(s + 2 * NS + sign * (1 + t), NS)
+        u = t // NY
+        dx = lax.rem(2 + 3 * u + 3 * (u * (u - 1) // 2), NX)
+        dy = NY - 1 - lax.rem(t, NY)
+        to_x = lax.rem(cx + NX + sign * dx, NX)
+        to_y = lax.rem(s // NX + NY + sign * dy, NY)
+        return to_y * NX + to_x
+
     def turn(t):
-        return lax.rem(s + 1 + t, NS)
+        return hop(t, 1)
 
     def origin(t):
-        return lax.rem(s + 2 * NS - 1 - t, NS)
+        return hop(t, -1)
+
+    def ring(n, i):
+        return min(i, n - i)
+
+    away_first = sorted(
+        ((dx, dy) for dx in range(NX) for dy in range(2 * NY) if dx or dy),
+        key=lambda o: -ring(NX, o[0]) - ring(2 * NY, o[1]),
+    )
+
+    def plane(offset):
+        to_x, to_y = lax.rem(cx + offset[0], NX), lax.rem(cy + offset[1], 2 * NY)
+        return lax.rem(to_y, NY) * NX + to_x, to_y // NY
 
     @pl.loop(0, NS)
     def _(t):
@@ -104,12 +131,6 @@
         @pl.loop(0, NS)
         def _(j):
             greet({"group": pgroup, "shard": j, "side": pside})
-
-        pl.semaphore_wait(barrier, NP - 1 + NZ - 1 + 1 + NS)
-
-    @pl.when(same)
-    def _():
-        pl.semaphore_wait(barrier, NP - 1 + NZ - 1 + 1)
 
     def a_copy(j):
         return remote(
@@ -126,15 +147,26 @@
         m = MOMENTUM_BETA * mom[j] + g
         mom[j] = m
         sbuf[j] = (g + MOMENTUM_BETA * m).astype(BF16)
-        own = jnp.logical_and(same, j == s)
-
-        @pl.when(own)
-        def _():
-            xbuf[rows_of(mine), :] = sbuf[j]
-
-        @pl.when(jnp.logical_not(own))
+
+    @pl.when(differ)
+    def _():
+        pl.semaphore_wait(barrier, NP - 1 + NZ - 1 + 1 + NS)
+
+    @pl.when(same)
+    def _():
+        pl.semaphore_wait(barrier, NP - 1 + NZ - 1 + 1)
+
+    @pl.loop(0, NS)
+    def _(t):
+        j = turn(t)
+
+        @pl.when(jnp.logical_not(jnp.logical_and(same, j == s)))
         def _():
             a_copy(j).start()
+
+    @pl.when(same)
+    def _():
+        xbuf[rows_of(mine), :] = sbuf[s]
 
     for c in w_loads:
         c.start()
@@ -210,26 +242,17 @@
         def _():
             gram(origin(t - 1))
 
-    gram(origin(NS - 1))
-
     def d_copy(j, h):
         return remote(
             mhalf.at[j, h], mbuf.at[rows_of(mine)], d_send.at[j * 2 + h], d_recv.at[mine],
             {"group": gi, "shard": j, "side": h},
         )
 
-    @pl.loop(0, NP)
-    def _(i):
-        r = lax.rem(mine + i, NP)
-        j, h = r // 2, lax.rem(r, 2)
-
-        @pl.when(i == 0)
-        def _():
-            mbuf[rows_of(mine), :] = mhalf[j, h]
-
-        @pl.when(i > 0)
-        def _():
-            d_copy(j, h).start()
+    for offset in away_first:
+        d_copy(*plane(offset)).start()
+    mbuf[rows_of(mine), :] = mhalf[s, a]
+
+    gram(origin(NS - 1))
 
     B = 128
     eye = lax.broadcasted_iota(jnp.int32, (B, B), 0) == lax.broadcasted_iota(jnp.int32, (B, B), 1)
@@ -363,51 +386,66 @@
         chosen[...], hidden, (((0,), (0,)), ((), ())), preferred_element_type=F32
     ).astype(BF16)
 
-    def share(core):
+    def rows_for(core):
         parts = [pl.ds(pl.multiple_of((i * 2 + core) * TB, TB), TB) for i in range(NZ)]
-        rows = jnp.concatenate([hid[p, :] for p in parts], axis=0)
-        return dot(rows, downw[...])
-
-    away = share(1 - k).astype(BF16)
-    for i in range(NZ):
-        e1send[i] = away[i * TB:(i + 1) * TB]
-    e1_copy = remote(e1send, e1recv, e1_s, e1_r, sibling)
-    e1_copy.start()
-    home = share(k)
-    for i in range(NZ):
-        e1own[i] = home[i * TB:(i + 1) * TB]
-    e1_copy.wait_recv()
-
-    def e2_copy(i):
+        return jnp.concatenate([hid[p, :] for p in parts], axis=0)
+
+    def e1_copy(c):
+        return remote(e1send.at[c], e1recv.at[c], e1_s.at[c], e1_r.at[c], sibling)
+
+    near = (z + 1 - 2 * lax.rem(z, 2), NZ - 1 - z)
+
+    def e2_copy(c, i):
+        peer = {"group": near[(c + i) % 2] * 2 + k, "shard": s, "side": a}
+        if i == 0:
+            return remote(e2send.at[c], e2recv.at[c], e2_s.at[c, 0], e2_r.at[c, 0], peer)
+        return remote(e2last.at[c], e2got.at[c], e2_s.at[c, 1], e2_r.at[c, 1], peer)
+
+    def e3_copy(c, j, h, slot):
+        r = j * 2 + h
         return remote(
-            e2send.at[i], e2recv.at[i], e2_s.at[i], e2_r.at[i],
-            {"group": lax.rem(z + 1 + i, NZ) * 2 + k, "shard": s, "side": a},
+            e3send.at[c, r], e3recv.at[c, slot], e3_s.at[c, r], e3_r.at[c, slot],
+            {"group": gi, "shard": j, "side": h},
         )
 
-    @pl.loop(0, NZ - 1)
-    def _(i):
-        to = lax.rem(z + 1 + i, NZ)
-        e2send[i] = (e1own[to] + e1recv[to].astype(F32)).astype(BF16)
-        e2_copy(i).start()
-
-    total = e1own[z] + e1recv[z].astype(F32)
-    for i in range(NZ - 1):
-        e2_copy(i).wait_recv()
-        total = total + e2recv[i].astype(F32)
-    for r in range(NP):
-        e3send[r] = total[r * RB:(r + 1) * RB].astype(BF16)
-
-    def e3_copy(r, slot):
-        return remote(
-            e3send.at[r], e3recv.at[slot], e3_s.at[r], e3_r.at[slot],
-            {"group": gi, "shard": r // 2, "side": lax.rem(r, 2)},
-        )
-
-    @pl.loop(1, NP)
-    def _(i):
-        e3_copy(lax.rem(mine + i, NP), mine).start()
-
-    e3recv[mine] = e3send[mine]
+    WIDE = D // CHUNKS
+    lanes = [slice(c * WIDE, (c + 1) * WIDE) for c in range(CHUNKS)]
+    rows = rows_for(1 - k)
+    for c in range(CHUNKS):
+        e1send[c] = dot(rows, downw[:, lanes[c]]).astype(BF16)
+        e1_copy(c).start()
+    rows = rows_for(k)
+    for c in range(CHUNKS):
+        e1own[c] = dot(rows, downw[:, lanes[c]])
+
+    def block(i):
+        return pl.ds(pl.multiple_of(i * TB, TB), TB)
+
+    def both(c, i):
+        return e1own[c, block(i), :] + e1recv[c, block(i), :].astype(F32)
+
+    for c in range(CHUNKS):
+        first, second = near[c % 2], near[(c + 1) % 2]
+        e1_copy(c).wait_recv()
+        e2send[c, 0] = both(c, first).astype(BF16)
+        e2send[c, 1] = both(c, NZ - 1 - first if c % 2 == 0 else first + 1 - 2 * lax.rem(first, 2)).astype(BF16)
+        e2_copy(c, 0).start()
+        e1own[c, block(z), :] = both(c, z)
+        e1own[c, block(second), :] = both(c, second)
+    for c in range(CHUNKS):
+        second = near[(c + 1) % 2]
+        e2_copy(c, 0).wait_recv()
+        e2last[c] = (e1own[c, block(second), :] + e2recv[c, 1].astype(F32)).astype(BF16)
+        e2_copy(c, 1).start()
+    for c in range(CHUNKS):
+        total = e1own[c, block(z), :] + e2recv[c, 0].astype(F32)
+        e2_copy(c, 1).wait_recv()
+        total = total + e2got[c].astype(F32)
+        for r in range(NP):
+            e3send[c, r] = total[r * RB:(r + 1) * RB].astype(BF16)
+        for offset in away_first:
+            e3_copy(c, *plane(offset), mine).start()
+        e3recv[c, mine] = e3send[c, mine]
 
     @pl.loop(0, NS)
     def _(t):
@@ -422,15 +460,16 @@
 
         mast[o] = decay * mast[o] - step_scale * obuf[o].astype(F32)
 
-    @pl.loop(1, NP)
-    def _(i):
-        r = lax.rem(mine + i, NP)
-        e3_copy(r, r).wait_recv()
-
-    final = e3recv[0].astype(F32)
-    for r in range(1, NP):
-        final = final + e3recv[r].astype(F32)
-    comb[...] = final.astype(BF16)
+    for c in range(CHUNKS):
+        @pl.loop(1, NP)
+        def _(i):
+            r = lax.rem(mine + i, NP)
+            e3_copy(c, r // 2, lax.rem(r, 2), r).wait_recv()
+
+        final = e3recv[c, 0].astype(F32)
+        for r in range(1, NP):
+            final = final + e3recv[c, r].astype(F32)
+        comb[:, lanes[c]] = final.astype(BF16)
 
     @pl.loop(0, NS)
     def _(t):
@@ -447,21 +486,25 @@
     def _(i):
         r = lax.rem(mine + i, NP)
         d_copy(r // 2, lax.rem(r, 2)).wait_send()
-        e3_copy(r, mine).wait_send()
-
-    @pl.loop(0, NZ - 1)
-    def _(i):
-        e2_copy(i).wait_send()
-
-    e1_copy.wait_send()
+        for c in range(CHUNKS):
+            e3_copy(c, r // 2, lax.rem(r, 2), mine).wait_send()
+
+    for c in range(CHUNKS):
+        e1_copy(c).wait_send()
+        e2_copy(c, 0).wait_send()
+        e2_copy(c, 1).wait_send()
 
     @pl.when(differ)
     def _():
         t_copy.wait_send()
 
 
-def hand_over(*refs):
-    copies = [pltpu.make_async_copy(refs[i], refs[3 + i], refs[6].at[i]) for i in range(3)]
+def hand_over(master, momentum, combined, out_master, out_momentum, out_combined, sems):
+    count = master.shape[0]
+    copies = [pltpu.make_async_copy(combined, out_combined, sems.at[2 * count])]
+    for j in range(count):
+        copies.append(pltpu.make_async_copy(master.at[j], out_master.at[j], sems.at[j]))
+        copies.append(pltpu.make_async_copy(momentum.at[j], out_momentum.at[j], sems.at[count + j]))
     for c in copies:
         c.start()
     for c in copies:
@@ -476,6 +519,7 @@
     NP = 2 * NS
     TB = T // (2 * NZ)
     RB = TB // NP
+    WIDE = D // CHUNKS
     dma = pltpu.SemaphoreType.DMA
     vmem = pltpu.VMEM
     scratch = dict(
@@ -488,14 +532,17 @@
         upw=vmem((H, D), BF16), downw=vmem((H, D), BF16), tok=vmem((T, D), BF16),
         tok_o=vmem((CAP, D), BF16), tok_r=vmem((CAP, D), BF16), upv=vmem((CAP, H), F32),
         hid=vmem((T, H), BF16), chosen=vmem((CAP, T), BF16),
-        e1own=vmem((NZ, TB, D), F32), e1send=vmem((NZ, TB, D), BF16), e1recv=vmem((NZ, TB, D), BF16),
-        e2send=vmem((NZ - 1, TB, D), BF16), e2recv=vmem((NZ - 1, TB, D), BF16),
-        e3send=vmem((NP, RB, D), BF16), e3recv=vmem((NP, RB, D), BF16),
+        e1own=vmem((CHUNKS, NZ * TB, WIDE), F32),
+        e1send=vmem((CHUNKS, NZ * TB, WIDE), BF16), e1recv=vmem((CHUNKS, NZ * TB, WIDE), BF16),
+        e2send=vmem((CHUNKS, 2, TB, WIDE), BF16), e2recv=vmem((CHUNKS, 2, TB, WIDE), BF16),
+        e2last=vmem((CHUNKS, TB, WIDE), BF16), e2got=vmem((CHUNKS, TB, WIDE), BF16),
+        e3send=vmem((CHUNKS, NP, RB, WIDE), BF16), e3recv=vmem((CHUNKS, NP, RB, WIDE), BF16),
         ld_m=dma((NS,)), ld_g=dma((NS,)), ld_x=dma((NS,)), ld_w=dma((3,)),
         a_send=dma((NS,)), a_recv=dma((NS,)), f_send=dma((NS,)), f_recv=dma((NS,)),
         d_send=dma((NP,)), d_recv=dma((NP,)), c_send=dma((NS,)), c_recv=dma((NS,)),
-        t_send=dma, t_recv=dma, e1_s=dma, e1_r=dma,
-        e2_s=dma((NZ - 1,)), e2_r=dma((NZ - 1,)), e3_s=dma((NP,)), e3_r=dma((NP,)),
+        t_send=dma, t_recv=dma, e1_s=dma((CHUNKS,)), e1_r=dma((CHUNKS,)),
+        e2_s=dma((CHUNKS, 2)), e2_r=dma((CHUNKS, 2)),
+        e3_s=dma((CHUNKS, NP)), e3_r=dma((CHUNKS, NP)),
     )
     hbm = pl.BlockSpec(memory_space=pl.ANY)
     local = pl.BlockSpec(memory_space=pltpu.VMEM)
@@ -519,7 +566,7 @@
         out_shape=tuple(jax.ShapeDtypeStruct(o.shape, o.dtype) for o in outs),
         in_specs=[hbm] * 3,
         out_specs=[hbm] * 3,
-        scratch_shapes=[dma((3,))],
+        scratch_shapes=[dma((2 * NS + 1,))],
         compiler_params=pltpu.CompilerParams(vmem_limit_bytes=1024 * 1024),
         name="hand_over",
     )(*outs)

time: 91.9 us -> 83 us (0.903)
  Pallas kernels: 90.9 us -> 81.6 us
    pallas_call x1, Pallas kernels: 88.1 us -> 78.8 us  [body(): pl.pallas_call(functools.partial(kernel, (NZ, NS, ROWS, F, D, T)), out_sh...]
where the time goes in v2:
time: 83 us; the launch traced here: 82.4 us
  Pallas kernels  81.6 us (98%)
    pallas_call x1, Pallas kernels, body(): pl.pallas_call(functools.partial(kernel, (NZ, NS, ROWS, F, D, T)), out_sh...  78.8 us
    pallas_call x1, Pallas kernels, body(): pl.pallas_call(hand_over, out_shape=tuple((jax.ShapeDtypeStruct(o.shape,...  2.79 us

profile of v2, /device:TPU:1, one launch (start us, length us, event | category | flops | bytes accessed | tf_op | source)
XLA Modules:
  0.0 82.4 jit_solution(4895504964908826473)
XLA Ops:
  0.6 78.8 %muon_rollout.1 = (f32[8,128,768]{2,1,0:T(8,128)S(1)}, f32[8,128,768]{2,1,0:T(8,128)S(1)}, bf16[4,2048]{1,0:T(4,128)(2,1)S(1)}) custom-call(f32[8,128,768]{2,1,0:T(8,128)} %master.1, f32[8,128,768]{2,1,0:T(8,128)} %momentum.1, bf16[8,128,768]{2,1,0:T(8,128)(2,1)} %gradient.1, bf16[1,384,2048]{2,1,0:T(8,128)(2,1)} %up_hbm.1, bf16[1,384,2048]{2,1,0:T(8,128)(2,1)} %down_hbm.1, ...), custom_call_target="tpu_custom_call" | custom-call | tf_op jit(solution)/shard_map/muon_rollout/pallas_call | solution.py:549
  79.4 2.8 %hand_over.1 = (f32[8,128,768]{2,1,0:T(8,128)}, f32[8,128,768]{2,1,0:T(8,128)}, bf16[4,2048]{1,0:T(4,128)(2,1)}) custom-call(f32[8,128,768]{2,1,0:T(8,128)S(1)} %get-tuple-element.6.master, f32[8,128,768]{2,1,0:T(8,128)S(1)} %get-tuple-element.7.momentum, bf16[4,2048]{1,0:T(4,128)(2,1)S(1)} %get-tuple-element.8.combined), custom_call_target="tpu_custom_call" | custom-call | tf_op jit(solution)/shard_map/hand_over/pallas_call | solution.py:564

commit v3 on v2

--- a/solution.py
+++ b/solution.py
@@ -11,6 +11,7 @@
 NS_ITERS = 5
 CAP = 128
 CHUNKS = 2
+PIECES = 1
 MOMENTUM_BETA = 0.95
 LEARN_RATE = 0.08
 WEIGHT_DECAY = 0.1
@@ -29,14 +30,14 @@
 
 def kernel(
     dims,
-    master, momentum, gradient, up_hbm, down_hbm, tokens_hbm, routes, route_weight,
-    mast, mom, comb,
-    grad, sbuf, xbuf, mhalf, mbuf, obuf, osend,
+    master, momentum, gradient, up_hbm, down_hbm, tokens_hbm, routes_hbm, route_weight_hbm,
+    mast, mom, comb, obuf,
+    grad, sbuf, xbuf, px_send, px_recv, py_send, py_recv, qx_send, qx_recv, qy_send, qy_recv, kept, places, tokc, osend,
     rf, rb, mb, tf, tb, qf, qb, tx, gx, gsend,
-    upw, downw, tok, tok_o, tok_r, upv, hid, chosen,
+    upw, downw, tok, routes, route_weight, tok_o, tok_r, upv, hid, chosen,
     e1own, e1send, e1recv, e2send, e2recv, e2last, e2got, e3send, e3recv,
     ld_m, ld_g, ld_x, ld_w,
-    a_send, a_recv, f_send, f_recv, d_send, d_recv, c_send, c_recv,
+    a_send, a_recv, f_send, f_recv, px_s, px_r, py_s, py_r, qx_s, qx_r, qy_s, qy_r, c_send, c_recv,
     t_send, t_recv, e1_s, e1_r, e2_s, e2_r, e3_s, e3_r,
 ):
     NZ, NS, ROWS, F, D, T = dims
@@ -108,6 +109,8 @@
         pltpu.make_async_copy(tokens_hbm, tok, ld_w.at[0]),
         pltpu.make_async_copy(up_hbm.at[0], upw, ld_w.at[1]),
         pltpu.make_async_copy(down_hbm.at[0], downw, ld_w.at[2]),
+        pltpu.make_async_copy(routes_hbm, routes, ld_w.at[3]),
+        pltpu.make_async_copy(route_weight_hbm, route_weight, ld_w.at[4]),
     ]
 
     barrier = pltpu.get_barrier_semaphore()
@@ -132,15 +135,19 @@
         def _(j):
             greet({"group": pgroup, "shard": j, "side": pside})
 
-    def a_copy(j):
+    PART = ROWS // PIECES
+
+    def piece_of(r, u):
+        return pl.ds(pl.multiple_of(r * ROWS + u * PART, PART), PART)
+
+    def a_copy(j, u, row=mine, slot=s):
         return remote(
-            sbuf.at[j], xbuf.at[rows_of(mine)], a_send.at[j], a_recv.at[s],
+            sbuf.at[j, pl.ds(u * PART, PART)], xbuf.at[piece_of(row, u)],
+            a_send.at[j, u], a_recv.at[slot, u],
             {"group": pgroup, "shard": j, "side": pside},
         )
 
-    @pl.loop(0, NS)
-    def _(t):
-        j = turn(t)
+    def blend(j):
         pltpu.make_async_copy(momentum.at[j], mom.at[j], ld_m.at[j]).wait()
         pltpu.make_async_copy(gradient.at[j], grad.at[j], ld_g.at[j]).wait()
         g = grad[j].astype(F32)
@@ -148,6 +155,8 @@
         mom[j] = m
         sbuf[j] = (g + MOMENTUM_BETA * m).astype(BF16)
 
+    blend(turn(0))
+
     @pl.when(differ)
     def _():
         pl.semaphore_wait(barrier, NP - 1 + NZ - 1 + 1 + NS)
@@ -155,14 +164,21 @@
     @pl.when(same)
     def _():
         pl.semaphore_wait(barrier, NP - 1 + NZ - 1 + 1)
+
+    def partner(j):
+        return jnp.logical_not(jnp.logical_and(same, j == s))
 
     @pl.loop(0, NS)
     def _(t):
         j = turn(t)
 
-        @pl.when(jnp.logical_not(jnp.logical_and(same, j == s)))
+        @pl.when(t > 0)
         def _():
-            a_copy(j).start()
+            blend(j)
+
+        @pl.when(partner(j))
+        def _():
+            a_copy(j, 0).start()
 
     @pl.when(same)
     def _():
@@ -201,23 +217,98 @@
         tok_r[...], upw[...], (((1,), (1,)), ((), ())), preferred_element_type=F32
     )
 
+    HS = CAP // 2
+    NYT = 2 * NY
+    own_cols = pl.ds(pl.multiple_of(mine * ROWS, ROWS), ROWS)
+
+    named = [
+        jnp.max(jnp.where(routes[...] == gi * NS + j, 1.0, 0.0), axis=0, keepdims=True)
+        for j in range(NS)
+    ]
+    named = jnp.concatenate(named + [jnp.zeros((16 - NS, T), F32)], axis=0)
+    places[...] = jnp.where(named > 0.5, dot(named.astype(BF16), upper) - 1.0, -1.0)
+    tokc[...] = tok[:, own_cols]
+
     @pl.loop(0, NS)
     def _(t):
         j = turn(t)
         pltpu.make_async_copy(master.at[j], mast.at[j], ld_x.at[j]).wait()
-        half = mast[j].astype(BF16)
-        mhalf[j, 0] = half[:, :H]
-        mhalf[j, 1] = half[:, H:]
+        slot = lax.broadcasted_iota(jnp.int32, (CAP, T), 0).astype(F32)
+        taken = jnp.where(slot == places[pl.ds(j, 1), :], 1.0, 0.0).astype(BF16)
+        picked = dot(taken, tokc[...]).astype(BF16)
+        value = dot(picked, mast[j].astype(BF16)).astype(BF16)
+        to_x, to_y = lax.rem(j, NX), j // NX
+        px_send[to_x, to_y] = value[:HS, :H]
+        px_send[to_x, to_y + NY] = value[:HS, H:]
+        py_send[to_y, to_x] = value[HS:, :H]
+        py_send[to_y + NY, to_x] = value[HS:, H:]
+
+    def spot(offset):
+        j, h = plane(offset)
+        return {"group": gi, "shard": j, "side": h}
+
+    def px_copy(i):
+        src = px_send.at[lax.rem(cx + i, NX)]
+        return remote(src, px_recv.at[i - 1], px_s.at[i - 1], px_r.at[i - 1], spot((i, 0)))
+
+    def py_copy(i):
+        src = py_send.at[lax.rem(cy + i, NYT)]
+        return remote(src, py_recv.at[i - 1], py_s.at[i - 1], py_r.at[i - 1], spot((0, i)))
+
+    def qx_copy(i):
+        return remote(
+            qx_send.at[i - 1], qx_recv.at[i - 1], qx_s.at[i - 1], qx_r.at[i - 1], spot((0, i))
+        )
+
+    def qy_copy(i):
+        return remote(
+            qy_send.at[i - 1], qy_recv.at[i - 1], qy_s.at[i - 1], qy_r.at[i - 1], spot((i, 0))
+        )
+
+    def second_stage():
+        for i in range(1, NX):
+            px_copy(i).wait_recv()
+        for i in range(1, NYT):
+            py_copy(i).wait_recv()
+
+        def sum_x(y):
+            v = px_send[cx, y].astype(F32)
+            for i in range(NX - 1):
+                v = v + px_recv[i, y].astype(F32)
+            return v
+
+        def sum_y(x):
+            v = py_send[cy, x].astype(F32)
+            for i in range(NYT - 1):
+                v = v + py_recv[i, x].astype(F32)
+            return v
+
+        for i in range(1, NYT):
+            qx_send[i - 1] = sum_x(lax.rem(cy + i, NYT)).astype(BF16)
+            qx_copy(i).start()
+        for i in range(1, NX):
+            qy_send[i - 1] = sum_y(lax.rem(cx + i, NX)).astype(BF16)
+            qy_copy(i).start()
+        kept[:HS] = sum_x(cy)
+        kept[HS:] = sum_y(cx)
 
     rf[...] = jnp.zeros_like(rf)
     tx[...] = jnp.zeros_like(tx)
 
-    def f_copy(o, core):
-        block = rows_of(o * 2 + core)
-        return remote(xbuf.at[block], xbuf.at[block], f_send.at[o], f_recv.at[o], sibling)
+    def f_copy(o, u, core):
+        block = piece_of(o * 2 + core, u)
+        return remote(xbuf.at[block], xbuf.at[block], f_send.at[o, u], f_recv.at[o, u], sibling)
+
+    def arrive(o, u):
+        @pl.when(jnp.logical_not(jnp.logical_and(same, o == s)))
+        def _():
+            a_copy(o, u, o * 2 + k, o).wait_recv()
+
+        f_copy(o, u, k).start()
 
     def gram(o):
-        f_copy(o, 1 - k).wait_recv()
+        for u in range(PIECES):
+            f_copy(o, u, 1 - k).wait_recv()
         pair = pl.ds(pl.multiple_of(o * 2 * ROWS, 2 * ROWS), 2 * ROWS)
         x = xbuf[pair, :]
         rf[...] += lax.dot_general(
@@ -225,33 +316,29 @@
         )
         tx[...] += dot(tok_o[:, pair], x)
 
+    for u in range(PIECES - 1):
+        @pl.loop(0, NS)
+        def _(t):
+            arrive(origin(t), u)
+            j = turn(t)
+
+            @pl.when(partner(j))
+            def _():
+                a_copy(j, u).wait_send()
+                a_copy(j, u + 1).start()
+
     @pl.loop(0, NS)
     def _(t):
-        o = origin(t)
-
-        @pl.when(jnp.logical_not(jnp.logical_and(same, o == s)))
-        def _():
-            remote(
-                sbuf.at[o], xbuf.at[rows_of(o * 2 + k)], a_send.at[o], a_recv.at[o],
-                {"group": pgroup, "shard": o, "side": pside},
-            ).wait_recv()
-
-        f_copy(o, k).start()
+        arrive(origin(t), PIECES - 1)
 
         @pl.when(t > 0)
         def _():
             gram(origin(t - 1))
 
-    def d_copy(j, h):
-        return remote(
-            mhalf.at[j, h], mbuf.at[rows_of(mine)], d_send.at[j * 2 + h], d_recv.at[mine],
-            {"group": gi, "shard": j, "side": h},
-        )
-
-    for offset in away_first:
-        d_copy(*plane(offset)).start()
-    mbuf[rows_of(mine), :] = mhalf[s, a]
-
+    for i in range(1, NX):
+        px_copy(i).start()
+    for i in range(1, NYT):
+        py_copy(i).start()
     gram(origin(NS - 1))
 
     B = 128
@@ -324,12 +411,13 @@
         return d, q
 
     d, q = lax.fori_loop(1, NS_ITERS - 1, iteration, (d, q))
+    second_stage()
     d = recenter(d)
+    tx[...] = q * tx[...] + dot(tx[...].astype(BF16), qb[...])
     lead = form_mix(d)
-    q = grow_q(lead, q)
 
     cols = pl.ds(pl.multiple_of(k * H, H), H)
-    part = inverse * (q * tx[:, cols] + dot(tx[...].astype(BF16), qb[:, cols]))
+    part = inverse * (lead * tx[:, cols] + dot(tx[...].astype(BF16), mb[:, cols]))
     t_copy = remote(gsend, gx, t_send, t_recv, swap)
 
     @pl.when(same)
@@ -340,6 +428,8 @@
     def _():
         gsend[...] = part.astype(BF16)
         t_copy.start()
+
+    q = grow_q(lead, q)
 
     def c_copy(o):
         return remote(
@@ -364,23 +454,20 @@
             def _():
                 c_copy(o).start()
 
-    @pl.loop(1, NP)
-    def _(i):
-        r = lax.rem(mine + i, NP)
-        remote(
-            mhalf.at[r // 2, lax.rem(r, 2)], mbuf.at[rows_of(r)], d_send.at[r], d_recv.at[r],
-            {"group": gi, "shard": r // 2, "side": lax.rem(r, 2)},
-        ).wait_recv()
+    for i in range(1, NYT):
+        qx_copy(i).wait_recv()
+        kept[:HS] += qx_recv[i - 1].astype(F32)
+    for i in range(1, NX):
+        qy_copy(i).wait_recv()
+        kept[HS:] += qy_recv[i - 1].astype(F32)
 
     decay = 1.0 - LEARN_RATE * WEIGHT_DECAY
     step_scale = LEARN_RATE * 0.2 * math.sqrt(max(D, F))
-    kept = decay * dot(tok_r[...], mbuf[...])
-
     @pl.when(differ)
     def _():
         t_copy.wait_recv()
 
-    gate = kept - step_scale * gx[...].astype(F32)
+    gate = decay * kept[...] - step_scale * gx[...].astype(F32)
     hidden = (gate * (1.0 / (1.0 + jnp.exp(-gate))) * upv[...]).astype(BF16)
     hid[...] = lax.dot_general(
         chosen[...], hidden, (((0,), (0,)), ((), ())), preferred_element_type=F32
@@ -401,10 +488,10 @@
             return remote(e2send.at[c], e2recv.at[c], e2_s.at[c, 0], e2_r.at[c, 0], peer)
         return remote(e2last.at[c], e2got.at[c], e2_s.at[c, 1], e2_r.at[c, 1], peer)
 
-    def e3_copy(c, j, h, slot):
+    def e3_copy(j, h, slot):
         r = j * 2 + h
         return remote(
-            e3send.at[c, r], e3recv.at[c, slot], e3_s.at[c, r], e3_r.at[c, slot],
+            e3send.at[r], e3recv.at[slot], e3_s.at[r], e3_r.at[slot],
             {"group": gi, "shard": j, "side": h},
         )
 
@@ -442,10 +529,10 @@
         e2_copy(c, 1).wait_recv()
         total = total + e2got[c].astype(F32)
         for r in range(NP):
-            e3send[c, r] = total[r * RB:(r + 1) * RB].astype(BF16)
-        for offset in away_first:
-            e3_copy(c, *plane(offset), mine).start()
-        e3recv[c, mine] = e3send[c, mine]
+            e3send[r, :, lanes[c]] = total[r * RB:(r + 1) * RB].astype(BF16)
+    for offset in away_first:
+        e3_copy(*plane(offset), mine).start()
+    e3recv[mine] = e3send[mine]
 
     @pl.loop(0, NS)
     def _(t):
@@ -458,18 +545,16 @@
                 {"group": pgroup, "shard": o, "side": pside},
             ).wait_recv()
 
-        mast[o] = decay * mast[o] - step_scale * obuf[o].astype(F32)
-
-    for c in range(CHUNKS):
-        @pl.loop(1, NP)
-        def _(i):
-            r = lax.rem(mine + i, NP)
-            e3_copy(c, r // 2, lax.rem(r, 2), r).wait_recv()
-
-        final = e3recv[c, 0].astype(F32)
-        for r in range(1, NP):
-            final = final + e3recv[c, r].astype(F32)
-        comb[:, lanes[c]] = final.astype(BF16)
+
+    @pl.loop(1, NP)
+    def _(i):
+        r = lax.rem(mine + i, NP)
+        e3_copy(r // 2, lax.rem(r, 2), r).wait_recv()
+
+    final = e3recv[0].astype(F32)
+    for r in range(1, NP):
+        final = final + e3recv[r].astype(F32)
+    comb[...] = final.astype(BF16)
 
     @pl.loop(0, NS)
     def _(t):
@@ -477,18 +562,23 @@
 
         @pl.when(jnp.logical_not(jnp.logical_and(same, j == s)))
         def _():
-            a_copy(j).wait_send()
+            a_copy(j, PIECES - 1).wait_send()
             c_copy(j).wait_send()
 
-        f_copy(j, k).wait_send()
+        for u in range(PIECES):
+            f_copy(j, u, k).wait_send()
 
     @pl.loop(1, NP)
     def _(i):
         r = lax.rem(mine + i, NP)
-        d_copy(r // 2, lax.rem(r, 2)).wait_send()
-        for c in range(CHUNKS):
-            e3_copy(c, r // 2, lax.rem(r, 2), mine).wait_send()
-
+        e3_copy(r // 2, lax.rem(r, 2), mine).wait_send()
+
+    for i in range(1, NX):
+        px_copy(i).wait_send()
+        qy_copy(i).wait_send()
+    for i in range(1, NYT):
+        py_copy(i).wait_send()
+        qx_copy(i).wait_send()
     for c in range(CHUNKS):
         e1_copy(c).wait_send()
         e2_copy(c, 0).wait_send()
@@ -499,14 +589,18 @@
         t_copy.wait_send()
 
 
-def hand_over(master, momentum, combined, out_master, out_momentum, out_combined, sems):
-    count = master.shape[0]
-    copies = [pltpu.make_async_copy(combined, out_combined, sems.at[2 * count])]
+def hand_over(step_scale, mast, mom, comb, rows, out_master, out_momentum, out_combined, new, sems):
+    count = mast.shape[0]
+    copies = [pltpu.make_async_copy(comb, out_combined, sems.at[2 * count])]
     for j in range(count):
-        copies.append(pltpu.make_async_copy(master.at[j], out_master.at[j], sems.at[j]))
-        copies.append(pltpu.make_async_copy(momentum.at[j], out_momentum.at[j], sems.at[count + j]))
+        copies.append(pltpu.make_async_copy(mom.at[j], out_momentum.at[j], sems.at[count + j]))
     for c in copies:
         c.start()
+    for j in range(count):
+        new[j] = (1.0 - LEARN_RATE * WEIGHT_DECAY) * mast[j] - step_scale * rows[j].astype(F32)
+        c = pltpu.make_async_copy(new.at[j], out_master.at[j], sems.at[j])
+        c.start()
+        copies.append(c)
     for c in copies:
         c.wait()
 
@@ -520,29 +614,42 @@
     TB = T // (2 * NZ)
     RB = TB // NP
     WIDE = D // CHUNKS
+    NX = 4 if NS % 4 == 0 else NS
+    NYT = 2 * NS // NX
+    HS = CAP // 2
+    MX = max(1, NX - 1)
     dma = pltpu.SemaphoreType.DMA
     vmem = pltpu.VMEM
     scratch = dict(
         grad=vmem((NS, ROWS, F), BF16),
-        sbuf=vmem((NS, ROWS, F), BF16), xbuf=vmem((D, F), BF16), mhalf=vmem((NS, 2, ROWS, H), BF16),
-        mbuf=vmem((D, H), BF16), obuf=vmem((NS, ROWS, F), BF16), osend=vmem((NS, ROWS, F), BF16),
+        sbuf=vmem((NS, ROWS, F), BF16), xbuf=vmem((D, F), BF16),
+        px_send=vmem((NX, NYT, HS, H), BF16), px_recv=vmem((MX, NYT, HS, H), BF16),
+        py_send=vmem((NYT, NX, HS, H), BF16), py_recv=vmem((NYT - 1, NX, HS, H), BF16),
+        qx_send=vmem((NYT - 1, HS, H), BF16), qx_recv=vmem((NYT - 1, HS, H), BF16),
+        qy_send=vmem((MX, HS, H), BF16), qy_recv=vmem((MX, HS, H), BF16), kept=vmem((CAP, H), F32),
+        places=vmem((16, T), F32), tokc=vmem((T, ROWS), BF16),
+        osend=vmem((NS, ROWS, F), BF16),
         rf=vmem((F, F), F32), rb=vmem((F, F), BF16), mb=vmem((F, F), BF16), tf=vmem((F, F), F32),
         tb=vmem((F, F), BF16), qf=vmem((F, F), F32), qb=vmem((F, F), BF16), tx=vmem((CAP, F), F32),
         gx=vmem((CAP, H), BF16), gsend=vmem((CAP, H), BF16),
         upw=vmem((H, D), BF16), downw=vmem((H, D), BF16), tok=vmem((T, D), BF16),
+        routes=vmem(routes.T.shape, jnp.int32), route_weight=vmem(routes.T.shape, F32),
         tok_o=vmem((CAP, D), BF16), tok_r=vmem((CAP, D), BF16), upv=vmem((CAP, H), F32),
         hid=vmem((T, H), BF16), chosen=vmem((CAP, T), BF16),
         e1own=vmem((CHUNKS, NZ * TB, WIDE), F32),
         e1send=vmem((CHUNKS, NZ * TB, WIDE), BF16), e1recv=vmem((CHUNKS, NZ * TB, WIDE), BF16),
         e2send=vmem((CHUNKS, 2, TB, WIDE), BF16), e2recv=vmem((CHUNKS, 2, TB, WIDE), BF16),
         e2last=vmem((CHUNKS, TB, WIDE), BF16), e2got=vmem((CHUNKS, TB, WIDE), BF16),
-        e3send=vmem((CHUNKS, NP, RB, WIDE), BF16), e3recv=vmem((CHUNKS, NP, RB, WIDE), BF16),
-        ld_m=dma((NS,)), ld_g=dma((NS,)), ld_x=dma((NS,)), ld_w=dma((3,)),
-        a_send=dma((NS,)), a_recv=dma((NS,)), f_send=dma((NS,)), f_recv=dma((NS,)),
-        d_send=dma((NP,)), d_recv=dma((NP,)), c_send=dma((NS,)), c_recv=dma((NS,)),
+        e3send=vmem((NP, RB, D), BF16), e3recv=vmem((NP, RB, D), BF16),
+        ld_m=dma((NS,)), ld_g=dma((NS,)), ld_x=dma((NS,)), ld_w=dma((5,)),
+        a_send=dma((NS, PIECES)), a_recv=dma((NS, PIECES)),
+        f_send=dma((NS, PIECES)), f_recv=dma((NS, PIECES)),
+        px_s=dma((MX,)), px_r=dma((MX,)), py_s=dma((NYT - 1,)), py_r=dma((NYT - 1,)),
+        qx_s=dma((NYT - 1,)), qx_r=dma((NYT - 1,)), qy_s=dma((MX,)), qy_r=dma((MX,)),
+        c_send=dma((NS,)), c_recv=dma((NS,)),
         t_send=dma, t_recv=dma, e1_s=dma((CHUNKS,)), e1_r=dma((CHUNKS,)),
         e2_s=dma((CHUNKS, 2)), e2_r=dma((CHUNKS, 2)),
-        e3_s=dma((CHUNKS, NP)), e3_r=dma((CHUNKS, NP)),
+        e3_s=dma((NP,)), e3_r=dma((NP,)),
     )
     hbm = pl.BlockSpec(memory_space=pl.ANY)
     local = pl.BlockSpec(memory_space=pltpu.VMEM)
@@ -552,9 +659,10 @@
             vmem(master.shape, F32),
             vmem(master.shape, F32),
             vmem((RB, D), BF16),
+            vmem(master.shape, BF16),
         ),
-        in_specs=[hbm] * 6 + [local] * 2,
-        out_specs=[local] * 3,
+        in_specs=[hbm] * 8,
+        out_specs=[local] * 4,
         scratch_shapes=list(scratch.values()),
         compiler_params=pltpu.CompilerParams(
             collective_id=0, has_side_effects=True, vmem_limit_bytes=48 * 1024 * 1024
@@ -562,12 +670,12 @@
         name="muon_rollout",
     )(master, momentum, gradient, up_weight, down_weight, tokens, routes.T, route_weight.T)
     return pl.pallas_call(
-        hand_over,
-        out_shape=tuple(jax.ShapeDtypeStruct(o.shape, o.dtype) for o in outs),
-        in_specs=[hbm] * 3,
+        functools.partial(hand_over, LEARN_RATE * 0.2 * math.sqrt(max(D, F))),
+        out_shape=tuple(jax.ShapeDtypeStruct(o.shape, o.dtype) for o in outs[:3]),
+        in_specs=[local] * 4,
         out_specs=[hbm] * 3,
-        scratch_shapes=[dma((2 * NS + 1,))],
-        compiler_params=pltpu.CompilerParams(vmem_limit_bytes=1024 * 1024),
+        scratch_shapes=[vmem(master.shape, F32), dma((2 * NS + 1,))],
+        compiler_params=pltpu.CompilerParams(vmem_limit_bytes=8 * 1024 * 1024),
         name="hand_over",
     )(*outs)
 

time: 83 us -> 81.7 us (0.984)
    pallas_call x1, Pallas kernels: 78.8 us -> 78 us  [body(): pl.pallas_call(functools.partial(kernel, (NZ, NS, ROWS, F, D, T)), out_sh...]
where the time goes in v3:
time: 81.7 us; the launch traced here: 81.6 us
  Pallas kernels  80.8 us (99%)
    pallas_call x1, Pallas kernels, body(): pl.pallas_call(functools.partial(kernel, (NZ, NS, ROWS, F, D, T)), out_sh...  78 us
    pallas_call x1, Pallas kernels, body(): pl.pallas_call(functools.partial(hand_over, LEARN_RATE * 0.2 * math.sqrt(...  2.8 us

profile of v3, /device:TPU:1, one launch (start us, length us, event | category | flops | bytes accessed | tf_op | source)
XLA Modules:
  0.0 81.6 jit_solution(5727304926040158142)
XLA Ops:
  0.6 78.0 %muon_rollout.1 = (f32[8,128,768]{2,1,0:T(8,128)S(1)}, f32[8,128,768]{2,1,0:T(8,128)S(1)}, bf16[4,2048]{1,0:T(4,128)(2,1)S(1)}, bf16[8,128,768]{2,1,0:T(8,128)(2,1)S(1)}) custom-call(f32[8,128,768]{2,1,0:T(8,128)} %master.1, f32[8,128,768]{2,1,0:T(8,128)} %momentum.1, bf16[8,128,768]{2,1,0:T(8,128)(2,1)} %gradient.1, bf16[1,384,2048]{2,1,0:T(8,128)(2,1)} %up_hbm.1, ...), custom_call_target="tpu_custom_call" | custom-call | tf_op jit(solution)/shard_map/muon_rollout/pallas_call | solution.py:656
  78.6 2.8 %hand_over.1 = (f32[8,128,768]{2,1,0:T(8,128)}, f32[8,128,768]{2,1,0:T(8,128)}, bf16[4,2048]{1,0:T(4,128)(2,1)}) custom-call(f32[8,128,768]{2,1,0:T(8,128)S(1)} %get-tuple-element.7.mast, f32[8,128,768]{2,1,0:T(8,128)S(1)} %get-tuple-element.8.mom, bf16[4,2048]{1,0:T(4,128)(2,1)S(1)} %get-tuple-element.9.comb, bf16[8,128,768]{2,1,0:T(8,128)(2,1)S(1)} %get-tuple-element.10.rows), custom_call_target="tpu_custom_call" | custom-call | tf_op jit(solution)/shard_map/hand_over/pallas_call | solution.py:672
